TPU v7x, 32 devices: a whole 2x2x4 slice. The times are simulated.
32 devices in a mesh: dp: 4 (over y, core), row: 2 (over x), col: 4 (over z).
Axes of the slice: x: 2, y: 2, z: 4, core: 2. Of those that a mesh axis runs over, the one named last changes fastest.
Arguments:
- layer_input: bfloat16 [12288, 1536], P(('dp', 'col'), 'row'), may hold values from -6 to 6
- attn_gain: float32 [1536], P('row'), may hold values from 0.25 to 1.75
- qkv_weight: bfloat16 [1536, 4608], P('row', 'col'), may hold values from -0.15625 to 0.15625
- forget_weight: bfloat16 [1536, 24], P('row', 'col'), may hold values from -0.15625 to 0.15625
- forget_bias: float32 [24], P('col'), may hold values from 2.5 to 7
- out_weight: bfloat16 [1536, 1536], P('col', 'row'), may hold values from -0.625 to 0.625
- ffn_gain: float32 [1536], P('row'), may hold values from 0.25 to 1.75
- gate_weight: bfloat16 [1536, 4096], P('row', 'col'), may hold values from -0.15625 to 0.15625
- up_weight: bfloat16 [1536, 4096], P('row', 'col'), may hold values from -0.15625 to 0.15625
- down_weight: bfloat16 [4096, 1536], P('col', 'row'), may hold values from -0.09375 to 0.09375
- prompt_doc: int32 [8, 1024], P(('dp', 'row')), may hold values from 0 to 3, never falling along the last dimension, each value on 1 to 512 neighbouring positions
- branch_seg: int32 [8, 512], P(('dp', 'row')), may hold values from 0 to 3, never falling along the last dimension, each value on 1 to 256 neighbouring positions
- branch_doc: int32 [8, 4], P(('dp', 'row')), may hold values from 0 to 3
- out_cotangent: bfloat16 [12288, 1536], P(('dp', 'col'), 'row'), may hold values from -6 to 6
Outputs:
- layer_output: bfloat16 [12288, 1536], P(('dp', 'col'), 'row')
- input_grad: bfloat16 [12288, 1536], P(('dp', 'col'), 'row')
- attn_gain_grad: float32 [1536], P('row')
- qkv_grad: float32 [1536, 4608], P('row', 'col')
- forget_grad: float32 [1536, 24], P('row', 'col')
- forget_bias_grad: float32 [24], P('col')
- out_grad: float32 [1536, 1536], P('col', 'row')
- ffn_gain_grad: float32 [1536], P('row')
- gate_grad: float32 [1536, 4096], P('row', 'col')
- up_grad: float32 [1536, 4096], P('row', 'col')
- down_grad: float32 [4096, 1536], P('col', 'row')
Inputs may be any that keep to these rules, and one draw needn't show every extreme that they name: `prompt_doc`: in each group the prompt's documents are numbered 0 to 3 in order, every one present, each of 1 to 512 tokens, one of exactly 512. `branch_seg`: in each group the continuations are numbered 0 to 3 in order, every one present, each of 1 to 256 tokens, one of exactly 256.
All inputs are finite; a program needn't handle non-finite values.
Results may differ from a plain program's by a relative error of at most 0.023.
Values may be sent and summed in bfloat16 or wider, within the bound.
A program may use at most 192 MiB of HBM per device.

v0:
```python
import jax
import jax.numpy as jnp
from jax import lax
from jax.sharding import PartitionSpec as P

D = 1536
DH = 64
DOCS = 4
QBLK = 512
EPS = 1e-06
MASKED = -1e30


def visible(row_start, doc_query, branch_query, doc_key, branch_key):
    pos_query = row_start + jnp.arange(doc_query.shape[0], dtype=jnp.int32)
    pos_key = jnp.arange(doc_key.shape[0], dtype=jnp.int32)
    causal = pos_key[None, :] <= pos_query[:, None]
    same_doc = doc_query[:, None] == doc_key[None, :]
    same_branch = (branch_key[None, :] < 0) | (branch_query[:, None] == branch_key[None, :])
    return causal & same_doc & same_branch


def decay_sums(log_rates, prompt_ids, branch_ids, branch_docs):
    prompt_len = prompt_ids.shape[0]
    prompt_part = log_rates[:prompt_len]
    branch_part = log_rates[prompt_len:]
    prompt_sums = jnp.cumsum(prompt_part, axis=0)
    doc_range = jnp.arange(DOCS, dtype=jnp.int32)
    doc_last = jnp.sum((prompt_ids[None, :] <= doc_range[:, None]).astype(jnp.int32), axis=1) - 1
    at_last = jnp.arange(prompt_len, dtype=jnp.int32)[None, :] == doc_last[:, None]
    doc_totals = jnp.sum(jnp.where(at_last[:, :, None], prompt_sums[None], 0.0), axis=1)
    branch_range = jnp.arange(branch_docs.shape[0], dtype=jnp.int32)
    picked = branch_docs[:, None] == doc_range[None, :]
    branch_start = jnp.sum(jnp.where(picked[:, :, None], doc_totals[None], 0.0), axis=1)
    earlier = branch_ids[None, :] < branch_range[:, None]
    skipped = jnp.sum(jnp.where(earlier[:, :, None], branch_part[None], 0.0), axis=1)
    member = branch_ids[:, None] == branch_range[None, :]
    offsets = jnp.sum(jnp.where(member[:, :, None], (branch_start - skipped)[None], 0.0), axis=1)
    decay_sum = jnp.concatenate([prompt_sums, jnp.cumsum(branch_part, axis=0) + offsets], axis=0)
    branch_doc_ids = jnp.sum(jnp.where(member, branch_docs[None, :], 0), axis=1)
    doc_ids = jnp.concatenate([prompt_ids, branch_doc_ids])
    branch_tags = jnp.concatenate([jnp.full((prompt_len,), -1, jnp.int32), branch_ids])
    return (decay_sum, doc_ids, branch_tags)


def block_scores(query_block, key_rows, decay_query, decay_key, allowed):
    raw_scores = jnp.einsum(
        "qhd,khd->hqk", query_block, key_rows, preferred_element_type=jnp.float32
    )
    scores = raw_scores * DH ** (-0.5) + decay_query.T[:, :, None] - decay_key.T[:, None, :]
    return jnp.where(allowed[None], scores, MASKED)


def contract_rows(left, right):
    return lax.dot_general(
        left, right, (((0,), (0,)), ((), ())), preferred_element_type=jnp.float32
    )


def contract_cols(left, right):
    return lax.dot_general(
        left, right, (((1,), (1,)), ((), ())), preferred_element_type=jnp.float32
    )


def row_stat(values):
    return lax.psum(values, "row")


def gather_tokens(token_rows):
    return lax.all_gather(token_rows, "col", axis=0, tiled=True)


def sum_tokens(partial_value):
    return lax.psum_scatter(
        partial_value.astype(jnp.bfloat16), "col", scatter_dimension=0, tiled=True
    ).astype(jnp.float32)


def gather_group(group_rows):
    return lax.all_gather(group_rows, "row", axis=0, tiled=True)


def sum_group(partial_value):
    return lax.psum_scatter(
        partial_value.astype(jnp.bfloat16), "row", scatter_dimension=0, tiled=True
    ).astype(jnp.float32)


def sum_pair(first, second):
    return (
        lax.psum_scatter(first, "row", scatter_dimension=0, tiled=True),
        lax.psum_scatter(second, "row", scatter_dimension=0, tiled=True),
    )


def gather_pair(first, second):
    return (
        lax.all_gather(first, "row", axis=0, tiled=True),
        lax.all_gather(second, "row", axis=0, tiled=True),
    )


def shards(
    layer_input,
    attn_gain,
    qkv_weight,
    forget_weight,
    forget_bias,
    out_weight,
    ffn_gain,
    gate_weight,
    up_weight,
    down_weight,
    prompt_doc,
    branch_seg,
    branch_doc,
    out_cotangent,
):
    score_scale = DH ** (-0.5)
    stream = layer_input.astype(jnp.float32)
    rms_a = lax.rsqrt(row_stat(jnp.sum(stream * stream, axis=1)) / D + EPS)[:, None]
    normed_a = (stream * rms_a * attn_gain).astype(jnp.bfloat16)
    normed_a_all = gather_tokens(normed_a)
    projected, forget_sum = sum_pair(
        jnp.dot(normed_a_all, qkv_weight, preferred_element_type=jnp.float32),
        jnp.dot(normed_a_all, forget_weight, preferred_element_type=jnp.float32),
    )
    group_len = projected.shape[0]
    heads = forget_weight.shape[1]
    qkv = projected.astype(jnp.bfloat16).reshape(group_len, heads, 3, DH)
    forget_logit = forget_sum + forget_bias
    log_rate = jax.nn.log_sigmoid(forget_logit)
    prompt_ids = prompt_doc[0]
    branch_ids = branch_seg[0]
    branch_docs = branch_doc[0]
    decay_sum, doc_ids, branch_tags = decay_sums(log_rate, prompt_ids, branch_ids, branch_docs)
    queries = qkv[:, :, 0]
    key_rows = qkv[:, :, 1]
    value_rows = qkv[:, :, 2]
    blocks = jnp.arange(group_len // QBLK, dtype=jnp.int32)

    def block_view(block_index):
        row_start = block_index * QBLK
        query_block = lax.dynamic_slice_in_dim(queries, row_start, QBLK, 0)
        decay_query = lax.dynamic_slice_in_dim(decay_sum, row_start, QBLK, 0)
        doc_query = lax.dynamic_slice_in_dim(doc_ids, row_start, QBLK, 0)
        branch_query = lax.dynamic_slice_in_dim(branch_tags, row_start, QBLK, 0)
        allowed = visible(row_start, doc_query, branch_query, doc_ids, branch_tags)
        scores = block_scores(query_block, key_rows, decay_query, decay_sum, allowed)
        return (row_start, query_block, scores)

    def forward_block(block_index):
        row_start, query_block, scores = block_view(block_index)
        row_max = jnp.max(scores, axis=2, keepdims=True)
        expo = jnp.exp(scores - row_max)
        row_total = jnp.sum(expo, axis=2, keepdims=True)
        probs = (expo / row_total).astype(jnp.bfloat16)
        attended_block = jnp.einsum(
            "hqk,khd->qhd", probs, value_rows, preferred_element_type=jnp.float32
        ).astype(jnp.bfloat16)
        return (attended_block, (row_max + jnp.log(row_total))[:, :, 0])

    attended_blocks, lse_blocks = lax.map(forward_block, blocks)
    attended = attended_blocks.reshape(group_len, heads * DH)
    attended_all = gather_group(attended)
    branch_out = sum_tokens(jnp.dot(attended_all, out_weight, preferred_element_type=jnp.float32))
    resid = stream + branch_out
    rms_b = lax.rsqrt(row_stat(jnp.sum(resid * resid, axis=1)) / D + EPS)[:, None]
    normed_b = (resid * rms_b * ffn_gain).astype(jnp.bfloat16)
    normed_b_all = gather_tokens(normed_b)
    gate_pre, up_pre = sum_pair(
        jnp.dot(normed_b_all, gate_weight, preferred_element_type=jnp.float32),
        jnp.dot(normed_b_all, up_weight, preferred_element_type=jnp.float32),
    )
    gate_sig = jax.nn.sigmoid(gate_pre)
    gate_act = gate_pre * gate_sig
    hidden = (gate_act * up_pre).astype(jnp.bfloat16)
    hidden_all = gather_group(hidden)
    layer_output = (
        resid + sum_tokens(jnp.dot(hidden_all, down_weight, preferred_element_type=jnp.float32))
    ).astype(jnp.bfloat16)
    cotangent = out_cotangent.astype(jnp.float32)
    cotangent_all = gather_tokens(out_cotangent)
    down_grad = contract_rows(hidden_all, cotangent_all)
    grad_hidden = sum_group(contract_cols(cotangent_all, down_weight))
    grad_gate = (grad_hidden * up_pre * gate_sig * (1.0 + gate_pre * (1.0 - gate_sig))).astype(
        jnp.bfloat16
    )
    grad_up = (grad_hidden * gate_act).astype(jnp.bfloat16)
    grad_gate_all, grad_up_all = gather_pair(grad_gate, grad_up)
    gate_grad = contract_rows(normed_b_all, grad_gate_all)
    up_grad = contract_rows(normed_b_all, grad_up_all)
    grad_normed_b = sum_tokens(
        contract_cols(grad_gate_all, gate_weight) + contract_cols(grad_up_all, up_weight)
    )
    gained_b = ffn_gain * grad_normed_b
    inner_b = row_stat(jnp.sum(resid * gained_b, axis=1))[:, None]
    ffn_gain_part = jnp.sum(grad_normed_b * resid * rms_b, axis=0)
    grad_resid = cotangent + rms_b * gained_b - resid * (rms_b * rms_b * rms_b) * inner_b / D
    grad_branch = grad_resid.astype(jnp.bfloat16)
    grad_branch_all = gather_tokens(grad_branch)
    out_grad = contract_rows(attended_all, grad_branch_all)
    attended_part = contract_cols(grad_branch_all, out_weight)
    grad_attended = sum_group(attended_part).astype(jnp.bfloat16).reshape(group_len, heads, DH)

    def back_block(carry, block_index):
        key_acc, value_acc, decay_keys = carry
        row_start, query_block, scores = block_view(block_index)
        grad_block = lax.dynamic_slice_in_dim(grad_attended, row_start, QBLK, 0)
        lse_block = lax.dynamic_index_in_dim(lse_blocks, block_index, 0, keepdims=False)
        probs_star = jnp.exp(scores - lse_block[:, :, None])
        grad_probs = jnp.einsum(
            "qhd,khd->hqk", grad_block, value_rows, preferred_element_type=jnp.float32
        )
        row_delta = jnp.sum(probs_star * grad_probs, axis=2, keepdims=True)
        grad_scores = (probs_star * (grad_probs - row_delta)).astype(jnp.bfloat16)
        grad_query = (
            jnp.einsum("hqk,khd->qhd", grad_scores, key_rows, preferred_element_type=jnp.float32)
            * score_scale
        )
        key_acc = key_acc + jnp.einsum(
            "hqk,qhd->khd", grad_scores, query_block, preferred_element_type=jnp.float32
        )
        value_acc = value_acc + jnp.einsum(
            "hqk,qhd->khd",
            probs_star.astype(jnp.bfloat16),
            grad_block,
            preferred_element_type=jnp.float32,
        )
        decay_rows = jnp.sum(grad_scores, axis=2, dtype=jnp.float32)
        decay_keys = decay_keys - jnp.sum(grad_scores, axis=1, dtype=jnp.float32)
        return ((key_acc, value_acc, decay_keys), (grad_query, decay_rows))

    zero_rows = jnp.zeros((group_len, heads, DH), jnp.float32)
    carried, stacked = lax.scan(
        back_block, (zero_rows, zero_rows, jnp.zeros((heads, group_len), jnp.float32)), blocks
    )
    key_acc, value_acc, decay_keys = carried
    query_blocks, decay_blocks = stacked
    grad_query = query_blocks.reshape(group_len, heads, DH)
    grad_decay = jnp.transpose(decay_blocks, (0, 2, 1)).reshape(group_len, heads) + decay_keys.T
    grad_qkv = (
        jnp.stack([grad_query, key_acc * score_scale, value_acc], axis=2)
        .astype(jnp.bfloat16)
        .reshape(group_len, heads * 3 * DH)
    )
    unused, pullback = jax.vjp(
        lambda log_rates: decay_sums(log_rates, prompt_ids, branch_ids, branch_docs)[0], log_rate
    )
    grad_log_rate = pullback(grad_decay)[0]
    grad_forget = (grad_log_rate * jax.nn.sigmoid(-forget_logit)).astype(jnp.bfloat16)
    grad_qkv_all, grad_forget_all = gather_pair(grad_qkv, grad_forget)
    qkv_grad = contract_rows(normed_a_all, grad_qkv_all)
    forget_grad = contract_rows(normed_a_all, grad_forget_all)
    forget_bias_grad = jnp.sum(grad_forget_all, axis=0, dtype=jnp.float32)
    grad_normed_a = sum_tokens(
        contract_cols(grad_qkv_all, qkv_weight) + contract_cols(grad_forget_all, forget_weight)
    )
    gained_a = attn_gain * grad_normed_a
    inner_a = row_stat(jnp.sum(stream * gained_a, axis=1))[:, None]
    attn_gain_part = jnp.sum(grad_normed_a * stream * rms_a, axis=0)
    input_grad = (
        grad_resid + rms_a * gained_a - stream * (rms_a * rms_a * rms_a) * inner_a / D
    ).astype(jnp.bfloat16)
    attn_gain_grad, ffn_gain_grad = lax.psum((attn_gain_part, ffn_gain_part), ("dp", "col"))
    summed = (
        lax.psum(qkv_grad.astype(jnp.bfloat16), "dp").astype(jnp.float32),
        lax.psum(forget_grad.astype(jnp.bfloat16), "dp").astype(jnp.float32),
        lax.psum(forget_bias_grad.astype(jnp.bfloat16), "dp").astype(jnp.float32),
        lax.psum(out_grad.astype(jnp.bfloat16), "dp").astype(jnp.float32),
        lax.psum(gate_grad.astype(jnp.bfloat16), "dp").astype(jnp.float32),
        lax.psum(up_grad.astype(jnp.bfloat16), "dp").astype(jnp.float32),
        lax.psum(down_grad.astype(jnp.bfloat16), "dp").astype(jnp.float32),
    )
    return (
        layer_output,
        input_grad,
        attn_gain_grad,
        summed[0],
        summed[1],
        summed[2],
        summed[3],
        ffn_gain_grad,
        summed[4],
        summed[5],
        summed[6],
    )


def solution(mesh):
    in_specs = (
        P(("dp", "col"), "row"),
        P("row"),
        P("row", "col"),
        P("row", "col"),
        P("col"),
        P("col", "row"),
        P("row"),
        P("row", "col"),
        P("row", "col"),
        P("col", "row"),
        P(("dp", "row"), None),
        P(("dp", "row"), None),
        P(("dp", "row"), None),
        P(("dp", "col"), "row"),
    )
    out_specs = (
        P(("dp", "col"), "row"),
        P(("dp", "col"), "row"),
        P("row"),
        P("row", "col"),
        P("row", "col"),
        P("col"),
        P("col", "row"),
        P("row"),
        P("row", "col"),
        P("row", "col"),
        P("col", "row"),
    )
    return jax.shard_map(shards, mesh=mesh, in_specs=in_specs, out_specs=out_specs, check_vma=False)
```

profile of v0, /device:TPU:0, one launch (start us, length us, event | category | flops | bytes accessed | tf_op | source)
XLA Modules:
  0.0 2115.4 jit_solution(11031045359977941894)
XLA Ops:
  18.7 91.3 %all-gather.10.cloned.1.call-done = bf16[3072,768]{1,0:T(8,128)(2,1)} async-done(((bf16[768,768]{1,0:T(8,128)(2,1)}), bf16[3072,768]{1,0:T(8,128)(2,1)}) %all-gather.10.cloned.1.call-update) | async-done | bytes 4718608 | tf_op jit(solution)/shard_map/all_gather | solution.py:71
  132.6 154.2 %reduce-scatter.11.cloned.1.call-done = f32[1536,1152]{1,0:T(8,128)} async-done(((f32[3072,1152]{1,0:T(8,128)}), f32[1536,1152]{1,0:T(8,128)}) %reduce-scatter.11.cloned.1.call-update) | async-done | bytes 7077904 | tf_op jit(solution)/shard_map/reduce_scatter | solution.py:92
  301.6 77.2 %while.31 = (s32[]{:T(128)}, bf16[3,512,6,64]{1,3,2,0:T(8,128)(2,1)}, f32[3,6,512]{2,1,0:T(8,128)S(1)}, s32[3]{0:T(128)S(1)}, s32[1536]{0:T(1024)S(1)}, /*index=...) while((s32[]{:T(128)}, ...), condition=%wide.region_17.18_spmd, body=%wide.region_14.17_spmd.sunk | while | flops 1297808384 | bytes 66381052 | solution.py:164
  382.5 36.2 %all-gather.12.cloned.1.call-done = bf16[3072,384]{0,1:T(8,128)(2,1)} async-done(((bf16[1536,384]{0,1:T(8,128)(2,1)}), bf16[3072,384]{0,1:T(8,128)(2,1)}) %all-gather.12.cloned.1.call-update) | async-done | bytes 2359312 | tf_op jit(solution)/shard_map/all_gather | solution.py:81
  425.8 84.8 %reduce-scatter.15.cloned.1.call-done = bf16[768,768]{1,0:T(8,128)(2,1)} async-done(((bf16[3072,768]{1,0:T(8,128)(2,1)}), bf16[768,768]{1,0:T(8,128)(2,1)}) %reduce-scatter.15.cloned.1.call-update) | async-done | bytes 1179664 | tf_op jit(solution)/shard_map/reduce_scatter | solution.py:75
  520.1 81.9 %all-gather.18.cloned.1.call-done = bf16[3072,768]{1,0:T(8,128)(2,1)} async-done(((bf16[768,768]{1,0:T(8,128)(2,1)}), bf16[3072,768]{1,0:T(8,128)(2,1)}) %all-gather.18.cloned.1.call-update) | async-done | bytes 4718608 | tf_op jit(solution)/shard_map/all_gather | solution.py:71
  611.7 80.3 %all-gather.14.cloned.1.call-done = bf16[3072,768]{1,0:T(8,128)(2,1)} async-done(((bf16[768,768]{1,0:T(8,128)(2,1)}), bf16[3072,768]{1,0:T(8,128)(2,1)}) %all-gather.14.cloned.1.call-update) | async-done | bytes 4718608 | tf_op jit(solution)/shard_map/all_gather | solution.py:71
  712.6 57.2 %reduce-scatter.23.cloned.1.call-done = bf16[1536,1024]{1,0:T(8,128)(2,1)} async-done(((bf16[3072,1024]{1,0:T(8,128)(2,1)}), bf16[1536,1024]{1,0:T(8,128)(2,1)}) %reduce-scatter.23.cloned.1.call-update) | async-done | bytes 3145744 | tf_op jit(solution)/shard_map/reduce_scatter | solution.py:85
  769.9 146.9 %reduce-scatter.19.cloned.1.call-done = f32[1536,1024]{1,0:T(8,128)} async-done(((f32[3072,1024]{1,0:T(8,128)}), f32[1536,1024]{1,0:T(8,128)}) %reduce-scatter.19.cloned.1.call-update) | async-done | bytes 6291472 | tf_op jit(solution)/shard_map/reduce_scatter | solution.py:93
  916.8 146.7 %reduce-scatter.17.cloned.1.call-done = f32[1536,1024]{1,0:T(8,128)} async-done(((f32[3072,1024]{1,0:T(8,128)}), f32[1536,1024]{1,0:T(8,128)}) %reduce-scatter.17.cloned.1.call-update) | async-done | bytes 6291472 | tf_op jit(solution)/shard_map/reduce_scatter | solution.py:92
  1074.1 79.9 %all-gather.20.cloned.1.call-done = bf16[3072,1024]{1,0:T(8,128)(2,1)} async-done(((bf16[1536,1024]{1,0:T(8,128)(2,1)}), bf16[3072,1024]{1,0:T(8,128)(2,1)}) %all-gather.20.cloned.1.call-update) | async-done | bytes 6291472 | tf_op jit(solution)/shard_map/all_gather | solution.py:99
  1164.1 72.4 %all-gather.22.cloned.1.call-done = bf16[3072,1024]{1,0:T(8,128)(2,1)} async-done(((bf16[1536,1024]{1,0:T(8,128)(2,1)}), bf16[3072,1024]{1,0:T(8,128)(2,1)}) %all-gather.22.cloned.1.call-update) | async-done | bytes 6291472 | tf_op jit(solution)/shard_map/all_gather | solution.py:100
  1247.1 85.4 %reduce-scatter.25.cloned.1.call-done = bf16[768,768]{1,0:T(8,128)(2,1)} async-done(((bf16[3072,768]{1,0:T(8,128)(2,1)}), bf16[768,768]{1,0:T(8,128)(2,1)}) %reduce-scatter.25.cloned.1.call-update) | async-done | bytes 1179664 | tf_op jit(solution)/shard_map/reduce_scatter | solution.py:75
  1344.7 90.0 %all-gather.24.cloned.1.call-done = bf16[3072,768]{1,0:T(8,128)(2,1)} async-done(((bf16[768,768]{1,0:T(8,128)(2,1)}), bf16[3072,768]{1,0:T(8,128)(2,1)}) %all-gather.24.cloned.1.call-update) | async-done | bytes 4718608 | tf_op jit(solution)/shard_map/all_gather | solution.py:71
  1442.1 32.5 %reduce-scatter.27.cloned.1.call-done = bf16[1536,384]{1,0:T(8,128)(2,1)} async-done(((bf16[3072,384]{1,0:T(8,128)(2,1)}), bf16[1536,384]{1,0:T(8,128)(2,1)}) %reduce-scatter.27.cloned.1.call-update) | async-done | bytes 1179664 | tf_op jit(solution)/shard_map/reduce_scatter | solution.py:85
  1477.0 203.3 %while.32 = (s32[]{:T(128)}, f32[1536,6,64]{0,2,1:T(8,128)}, f32[1536,6,64]{0,2,1:T(8,128)}, f32[6,1536]{1,0:T(8,128)S(1)}, bf16[3,512,6,64]{1,3,2,0:T(8,128)(2,...) while((s32[]{:T(128)}, f32[1536,6,64]{0,2,1:T(8,128)}, ...), condition=%wide.region_33.34_spmd.clone, body=%wide.region_29.33_spmd.clone.sunk | while | flops 3093238784 | bytes 276796800 | solution.py:236
  1507.9 16.3 convert_reduce_fusion.4
  1574.0 16.3 convert_reduce_fusion.4
  1641.8 16.3 convert_reduce_fusion.4
  1734.3 46.6 %all-gather.26.cloned.1.call-done = bf16[3072,1152]{0,1:T(8,128)(2,1)} async-done(((bf16[1536,1152]{0,1:T(8,128)(2,1)}), bf16[3072,1152]{0,1:T(8,128)(2,1)}) %all-gather.26.cloned.1.call-update) | async-done | bytes 7077904 | tf_op jit(solution)/shard_map/all_gather | solution.py:99
  1844.6 81.0 %all-reduce.8.cloned.1.call-done = (bf16[768,1152]{1,0:T(8,128)(2,1)}, bf16[384,768]{1,0:T(8,128)(2,1)}, bf16[768,1024]{1,0:T(8,128)(2,1)}, bf16[768,1024]{1,0:T(8,128)(2,1)}, bf16[1024,768]{1,0:T(8,128)(2,1)}) async-done(((bf16[768,1152]{1,0:T(8,128)(2,1)}, bf16[384,768]{1,0:T(8,128)(2,1)}, bf16[768,1024]{1,0:T(8,128)(2,1)}, bf16[768,1024]{1,0:T(8,128)(2,1)}, bf16[1024,768]{1,0:T(8,128)(2,1)}), ...) | async-done | bytes 7077904 | tf_op jit(solution)/shard_map/psum | solution.py:268
  1935.9 77.4 %reduce-scatter.29.cloned.1.call-done = bf16[768,768]{1,0:T(8,128)(2,1)} async-done(((bf16[3072,768]{1,0:T(8,128)(2,1)}), bf16[768,768]{1,0:T(8,128)(2,1)}) %reduce-scatter.29.cloned.1.call-update) | async-done | bytes 1179664 | tf_op jit(solution)/shard_map/reduce_scatter | solution.py:75
  2015.7 36.5 %all-reduce.3 = (f32[768]{0:T(1024)}, f32[768]{0:T(1024)}) all-reduce(f32[768]{0:T(1024)S(1)} %get-tuple-element.219, f32[768]{0:T(1024)S(1)} %copy-done.35), channel_id=1, replica_groups=mesh['dp'=4,'row'=2,'col'=4] {'dp','col'}, use_global_device_ids=true, to_apply=%region_46.47 | all-reduce | flops 1536 | bytes 12288 | tf_op jit(solution)/shard_map/psum | solution.py:266
  2057.1 46.4 %reduce-scatter.21.cloned.1.call-done = bf16[768,768]{1,0:T(8,128)(2,1)} async-done(((bf16[3072,768]{1,0:T(8,128)(2,1)}), bf16[768,768]{1,0:T(8,128)(2,1)}) %reduce-scatter.21.cloned.1.call-update) | async-done | bytes 1179664 | tf_op jit(solution)/shard_map/reduce_scatter | solution.py:75
  (351 shorter events, 513.4 us)
Async XLA Ops:
  7.2 102.8 %all-gather.10.cloned.1.call-start = ((), (), s32[]{:S(2)}) async-start(), calls=%async_computation.10 | async-start | bytes 5898240 | tf_op jit(solution)/shard_map/all_gather | solution.py:71
  18.6 108.0 %reduce-scatter.13.cloned.1.call-start = ((), (), s32[]{:S(2)}) async-start(), calls=%async_computation.12 | async-start | bytes 147456 | tf_op jit(solution)/shard_map/reduce_scatter | solution.py:93
  114.3 172.5 %reduce-scatter.11.cloned.1.call-start = ((), (), s32[]{:S(2)}) async-start(), calls=%async_computation.11 | async-start | bytes 21233664 | tf_op jit(solution)/shard_map/reduce_scatter | solution.py:92
  125.5 293.2 %all-gather.12.cloned.1.call-start = ((), (), s32[]{:S(2)}) async-start(), calls=%async_computation.13 | async-start | bytes 3538944 | tf_op jit(solution)/shard_map/all_gather | solution.py:81
  382.5 128.1 %reduce-scatter.15.cloned.1.call-start = ((), (), s32[]{:S(2)}) async-start(), calls=%async_computation.14 | async-start | bytes 5898240 | tf_op jit(solution)/shard_map/reduce_scatter | solution.py:75
  425.2 176.8 %all-gather.18.cloned.1.call-start = ((), (), s32[]{:S(2)}) async-start(), calls=%async_computation.20 | async-start | bytes 5898240 | tf_op jit(solution)/shard_map/all_gather | solution.py:71
  425.8 266.3 %all-gather.14.cloned.1.call-start = ((), (), s32[]{:S(2)}) async-start(), calls=%async_computation.15 | async-start | bytes 5898240 | tf_op jit(solution)/shard_map/all_gather | solution.py:71
  517.3 823.4 %copy-start.14 = (f32[768]{0:T(1024)}, f32[768]{0:T(1024)S(1)}, u32[]{:S(2)}) copy-start(f32[768]{0:T(1024)S(1)} %get-tuple-element.300) | copy-start | bytes 9220
  517.3 823.4 %copy-start.25 = (f32[768]{0:T(1024)}, f32[768]{0:T(1024)S(1)}, u32[]{:S(2)}) copy-start(f32[768]{0:T(1024)S(1)} %get-tuple-element.299) | copy-start | bytes 9220
  520.1 249.8 %reduce-scatter.23.cloned.1.call-start = ((), (), s32[]{:S(2)}) async-start(), calls=%async_computation.21 | async-start | bytes 9437184 | tf_op jit(solution)/shard_map/reduce_scatter | solution.py:85
  611.7 305.1 %reduce-scatter.19.cloned.1.call-start = ((), (), s32[]{:S(2)}) async-start(), calls=%async_computation.17 | async-start | bytes 18874368 | tf_op jit(solution)/shard_map/reduce_scatter | solution.py:93
  702.1 361.5 %reduce-scatter.17.cloned.1.call-start = ((), (), s32[]{:S(2)}) async-start(), calls=%async_computation.16 | async-start | bytes 18874368 | tf_op jit(solution)/shard_map/reduce_scatter | solution.py:92
  712.6 441.4 %all-gather.20.cloned.1.call-start = ((), (), s32[]{:S(2)}) async-start(), calls=%async_computation.22 | async-start | bytes 9437184 | tf_op jit(solution)/shard_map/all_gather | solution.py:99
  1073.5 163.0 %all-gather.22.cloned.1.call-start = ((), (), s32[]{:S(2)}) async-start(), calls=%async_computation.23 | async-start | bytes 9437184 | tf_op jit(solution)/shard_map/all_gather | solution.py:100
  1074.1 258.4 %reduce-scatter.25.cloned.1.call-start = ((), (), s32[]{:S(2)}) async-start(), calls=%async_computation.24 | async-start | bytes 5898240 | tf_op jit(solution)/shard_map/reduce_scatter | solution.py:75
  1247.1 187.7 %all-gather.24.cloned.1.call-start = ((), (), s32[]{:S(2)}) async-start(), calls=%async_computation.25 | async-start | bytes 5898240 | tf_op jit(solution)/shard_map/all_gather | solution.py:71
  1344.7 130.0 %reduce-scatter.27.cloned.1.call-start = ((), (), s32[]{:S(2)}) async-start(), calls=%async_computation.26 | async-start | bytes 3538944 | tf_op jit(solution)/shard_map/reduce_scatter | solution.py:85
  1441.3 269.8 %all-gather.16.cloned.1.call-start = ((), (), s32[]{:S(2)}) async-start(), calls=%async_computation.18 | async-start | bytes 9437184 | tf_op jit(solution)/shard_map/all_gather | solution.py:81
  1441.9 338.9 %all-gather.26.cloned.1.call-start = ((), (), s32[]{:S(2)}) async-start(), calls=%async_computation.27 | async-start | bytes 10616832 | tf_op jit(solution)/shard_map/all_gather | solution.py:99
  1691.1 234.5 %all-reduce.8.cloned.1.call-start = ((), (), s32[]{:S(2)}) async-start(), calls=%async_computation.29 | async-start | bytes 14155776 | tf_op jit(solution)/shard_map/psum | solution.py:268
  1792.0 221.3 %reduce-scatter.29.cloned.1.call-start = ((), (), s32[]{:S(2)}) async-start(), calls=%async_computation.28 | async-start | bytes 5898240 | tf_op jit(solution)/shard_map/reduce_scatter | solution.py:75
  1817.4 286.2 %reduce-scatter.21.cloned.1.call-start = ((), (), s32[]{:S(2)}) async-start(), calls=%async_computation.19 | async-start | bytes 5898240 | tf_op jit(solution)/shard_map/reduce_scatter | solution.py:75
  1935.9 167.6 %copy-start.19 = (f32[768]{0:T(1024)S(1)}, f32[768]{0:T(1024)}, u32[]{:S(2)}) copy-start(f32[768]{0:T(1024)} %param.24) | copy-start | bytes 9220
  1935.9 167.6 %copy-start.26 = (f32[768]{0:T(1024)S(1)}, f32[768]{0:T(1024)}, u32[]{:S(2)}) copy-start(f32[768]{0:T(1024)} %copy-done.25) | copy-start | bytes 9220
  (49 other events, 1676.4 us)
Sparse Core Ops, SparseCore 0:
  18.7 91.2 all-gather.9
  114.4 8.4 reduce-scatter.12
  125.6 161.1 reduce-scatter.10
  382.6 36.0 all-gather.11
  425.3 85.2 reduce-scatter.14
  512.0 89.9 all-gather.17
  604.1 87.8 all-gather.13
  694.3 75.5 reduce-scatter.22
  772.3 144.4 reduce-scatter.18
  919.1 144.4 reduce-scatter.16
  1073.6 80.3 all-gather.19
  1156.1 80.3 all-gather.21
  1247.2 85.2 reduce-scatter.24
  1344.8 89.9 all-gather.23
  1441.5 33.1 reduce-scatter.26
  1476.6 80.3 all-gather.15
  1691.2 89.5 all-gather.25
  1792.2 133.3 all-reduce.7
  1927.9 85.4 reduce-scatter.28
  2015.5 87.9 reduce-scatter.20
where the time goes:
time: 2120 us
  waiting for transfers between devices  1490 us (70%)
  matrix products  325 us (15%)
  other arithmetic  153 us (7%)
  blocking collectives  73.6 us (3%)
  local copies, waits for them, and re-layouts  44.4 us (2%)
    all_gather x4, waiting for transfers between devices, gather_tokens(): return lax.all_gather(token_rows, 'col', axis=0, tiled=True)  344 us
    reduce_scatter x2, waiting for transfers between devices, sum_pair(): lax.psum_scatter(first, 'row', scatter_dimension=0, tiled=True)  301 us
    reduce_scatter x4, waiting for transfers between devices, sum_tokens(): lax.psum_scatter(partial_value.astype(jnp.bfloat16), 'col', scatter_dimen...  294 us
    reduce_scatter x2, waiting for transfers between devices, sum_pair(): lax.psum_scatter(second, 'row', scatter_dimension=0, tiled=True)  147 us
    all_gather x2, waiting for transfers between devices, gather_pair(): lax.all_gather(first, 'row', axis=0, tiled=True)  127 us
    reduce_scatter x2, waiting for transfers between devices, sum_group(): lax.psum_scatter(partial_value.astype(jnp.bfloat16), 'row', scatter_dimen...  89.7 us
    psum x1, waiting for transfers between devices, shards(): lax.psum(qkv_grad.astype(jnp.bfloat16), 'dp').astype(jnp.float32)  81 us
    all_gather x1, waiting for transfers between devices, gather_pair(): lax.all_gather(second, 'row', axis=0, tiled=True)  72.4 us
  transfers between devices with their start and end apart: 20, of which 18 were waited for; matrix products, arithmetic and copies ran while one was open for 16% of the time, Pallas kernels for 0%

commit v1 on v0

--- a/solution.py
+++ b/solution.py
@@ -9,6 +9,22 @@
 QBLK = 512
 EPS = 1e-06
 MASKED = -1e30
+
+
+def gather_around(x, axis, dim):
+    ways, here, lap = (lax.axis_size(axis), lax.axis_index(axis), x.shape[dim])
+    lengths = [n * ways if d == dim else n for d, n in enumerate(x.shape)]
+    full = lax.dynamic_update_slice_in_dim(jnp.zeros(lengths, x.dtype), x, here * lap, axis=dim)
+    going_up = going_down = x
+    for far in range(1, ways // 2 + 1):
+        going_up = lax.ppermute(going_up, axis, [(d, (d + 1) % ways) for d in range(ways)])
+        full = lax.dynamic_update_slice_in_dim(full, going_up, (here - far) % ways * lap, axis=dim)
+        if 2 * far < ways:
+            going_down = lax.ppermute(going_down, axis, [(d, (d - 1) % ways) for d in range(ways)])
+            full = lax.dynamic_update_slice_in_dim(
+                full, going_down, (here + far) % ways * lap, axis=dim
+            )
+    return full
 
 
 def visible(row_start, doc_query, branch_query, doc_key, branch_key):
@@ -68,7 +84,7 @@
 
 
 def gather_tokens(token_rows):
-    return lax.all_gather(token_rows, "col", axis=0, tiled=True)
+    return gather_around(token_rows, "col", 0)
 
 
 def sum_tokens(partial_value):

time: 2120 us -> 2010 us (0.948)
  waiting for transfers between devices: 1490 us -> 1270 us
  starting transfers between devices: 1 us -> 110 us
  local copies, waits for them, and re-layouts: 44.4 us -> 65.8 us
    all_gather x4 -> x0, waiting for transfers between devices: 344 us -> none  [gather_tokens(): return lax.all_gather(token_rows, 'col', axis=0, tiled=True)]
    ppermute x0 -> x12, waiting for transfers between devices: none -> 273 us  [the longest x8 241 us: gather_around(): lax.ppermute(going_up, axis, [(d, (d + 1) % ways) for d in range(ways)])]
    ppermute x0 -> x12, starting transfers between devices: none -> 110 us  [the longest x8 99.7 us: gather_around(): lax.ppermute(going_up, axis, [(d, (d + 1) % ways) for d in range(ways)])]
    reduce_scatter x4, waiting for transfers between devices: 294 us -> 207 us  [sum_tokens(): lax.psum_scatter(partial_value.astype(jnp.bfloat16), 'col', scatter_dimen...]
    reduce_scatter x2, waiting for transfers between devices: 89.7 us -> 32.9 us  [sum_group(): lax.psum_scatter(partial_value.astype(jnp.bfloat16), 'row', scatter_dimen...]
  transfers between devices with their start and end apart: 20 -> 28, of which waited for: 18 -> 24; matrix products, arithmetic and copies ran while one was open for 16% -> 17% of each run, Pallas kernels for 0% -> 0%
where the time goes in v1:
time: 2010 us
  waiting for transfers between devices  1270 us (63%)
  matrix products  318 us (16%)
  other arithmetic  148 us (7%)
  starting transfers between devices  110 us (5%)
  blocking collectives  73.6 us (4%)
  local copies, waits for them, and re-layouts  65.8 us (3%)
    reduce_scatter x2, waiting for transfers between devices, sum_pair(): lax.psum_scatter(first, 'row', scatter_dimension=0, tiled=True)  302 us
    ppermute x8, waiting for transfers between devices, gather_around(): lax.ppermute(going_up, axis, [(d, (d + 1) % ways) for d in range(ways)])  241 us
    reduce_scatter x4, waiting for transfers between devices, sum_tokens(): lax.psum_scatter(partial_value.astype(jnp.bfloat16), 'col', scatter_dimen...  207 us
    reduce_scatter x2, waiting for transfers between devices, sum_pair(): lax.psum_scatter(second, 'row', scatter_dimension=0, tiled=True)  132 us
    all_gather x2, waiting for transfers between devices, gather_pair(): lax.all_gather(first, 'row', axis=0, tiled=True)  126 us
    ppermute x8, starting transfers between devices, gather_around(): lax.ppermute(going_up, axis, [(d, (d + 1) % ways) for d in range(ways)])  99.7 us
    psum x1, waiting for transfers between devices, shards(): lax.psum(qkv_grad.astype(jnp.bfloat16), 'dp').astype(jnp.float32)  81 us
    all_gather x1, waiting for transfers between devices, gather_pair(): lax.all_gather(second, 'row', axis=0, tiled=True)  72.6 us
  transfers between devices with their start and end apart: 28, of which 24 were waited for; matrix products, arithmetic and copies ran while one was open for 17% of the time, Pallas kernels for 0%

profile of v1, /device:TPU:0, one launch (start us, length us, event | category | flops | bytes accessed | tf_op | source)
XLA Modules:
  0.0 2006.2 jit_solution(18038580967893550883)
XLA Ops:
  23.5 27.1 %collective-permute-done = bf16[768,768]{1,0:T(8,128)(2,1)S(1)} collective-permute-done((bf16[768,768]{1,0:T(8,128)(2,1)}, bf16[768,768]{1,0:T(8,128)(2,1)S(1)}, u32[]{:S(2)}, u32[]{:S(2)}) %collective-permute-start) | collective-permute-done | bytes 1179680 | tf_op jit(solution)/shard_map/ppermute | solution.py:20
  77.1 22.1 %collective-permute-done.2 = bf16[768,768]{1,0:T(8,128)(2,1)} collective-permute-done((bf16[768,768]{1,0:T(8,128)(2,1)S(1)}, bf16[768,768]{1,0:T(8,128)(2,1)}, u32[]{:S(2)}, u32[]{:S(2)}) %collective-permute-start.2) | collective-permute-done | bytes 1179680 | tf_op jit(solution)/shard_map/ppermute | solution.py:20
  124.2 155.0 %reduce-scatter.11.cloned.1.call-done = f32[1536,1152]{1,0:T(8,128)} async-done(((f32[3072,1152]{1,0:T(8,128)}), f32[1536,1152]{1,0:T(8,128)}) %reduce-scatter.11.cloned.1.call-update) | async-done | bytes 7077904 | tf_op jit(solution)/shard_map/reduce_scatter | solution.py:108
  294.0 77.2 %while.31 = (s32[]{:T(128)}, bf16[3,512,6,64]{1,3,2,0:T(8,128)(2,1)}, f32[3,6,512]{2,1,0:T(8,128)S(1)}, s32[3]{0:T(128)S(1)}, s32[1536]{0:T(1024)S(1)}, /*index=...) while((s32[]{:T(128)}, ...), condition=%wide.region_17.18_spmd, body=%wide.region_14.17_spmd.sunk | while | flops 1297808384 | bytes 66381052 | solution.py:180
  374.9 36.2 %all-gather.6.cloned.1.call-done = bf16[3072,384]{0,1:T(8,128)(2,1)} async-done(((bf16[1536,384]{0,1:T(8,128)(2,1)}), bf16[3072,384]{0,1:T(8,128)(2,1)}) %all-gather.6.cloned.1.call-update) | async-done | bytes 2359312 | tf_op jit(solution)/shard_map/all_gather | solution.py:97
  422.7 48.7 %collective-permute-done.6 = bf16[768,768]{1,0:T(8,128)(2,1)S(1)} collective-permute-done((bf16[768,768]{1,0:T(8,128)(2,1)S(1)}, bf16[768,768]{1,0:T(8,128)(2,1)S(1)}, u32[]{:S(2)}, u32[]{:S(2)}) %collective-permute-start.6) | collective-permute-done | bytes 1179680 | tf_op jit(solution)/shard_map/ppermute | solution.py:20
  471.4 31.0 %collective-permute-start.8 = (bf16[768,768]{1,0:T(8,128)(2,1)S(1)}, bf16[768,768]{1,0:T(8,128)(2,1)S(1)}, u32[]{:S(2)}, u32[]{:S(2)}) collective-permute-start(bf16[768,768]{1,0:T(8,128)(2,1)S(1)} %collective-permute-done.6), channel_id=1, source_target_pairs={{0,1},{1,2},{2,3},{3,0},{4,5},{5,6},{6,7},{7,4},{8,9},{9,10},{10,1... | collective-permute-start | bytes 3538952 | tf_op jit(solution)/shard_map/ppermute | solution.py:20
  502.9 24.6 %collective-permute-done.7 = bf16[768,768]{1,0:T(8,128)(2,1)S(1)} collective-permute-done((bf16[768,768]{1,0:T(8,128)(2,1)S(1)}, bf16[768,768]{1,0:T(8,128)(2,1)S(1)}, u32[]{:S(2)}, u32[]{:S(2)}) %collective-permute-start.7) | collective-permute-done | bytes 1179680 | tf_op jit(solution)/shard_map/ppermute | solution.py:23
  527.6 43.8 %collective-permute-done.8 = bf16[768,768]{1,0:T(8,128)(2,1)S(1)} collective-permute-done((bf16[768,768]{1,0:T(8,128)(2,1)S(1)}, bf16[768,768]{1,0:T(8,128)(2,1)S(1)}, u32[]{:S(2)}, u32[]{:S(2)}) %collective-permute-start.8) | collective-permute-done | bytes 1179680 | tf_op jit(solution)/shard_map/ppermute | solution.py:20
  594.7 26.9 %collective-permute-done.3 = bf16[768,768]{1,0:T(8,128)(2,1)S(1)} collective-permute-done((bf16[768,768]{1,0:T(8,128)(2,1)S(1)}, bf16[768,768]{1,0:T(8,128)(2,1)S(1)}, u32[]{:S(2)}, u32[]{:S(2)}) %collective-permute-start.3) | collective-permute-done | bytes 1179680 | tf_op jit(solution)/shard_map/ppermute | solution.py:20
  687.5 132.4 %reduce-scatter.19.cloned.1.call-done = f32[1536,1024]{1,0:T(8,128)} async-done(((f32[3072,1024]{1,0:T(8,128)}), f32[1536,1024]{1,0:T(8,128)}) %reduce-scatter.19.cloned.1.call-update) | async-done | bytes 6291472 | tf_op jit(solution)/shard_map/reduce_scatter | solution.py:109
  819.9 146.9 %reduce-scatter.17.cloned.1.call-done = f32[1536,1024]{1,0:T(8,128)} async-done(((f32[3072,1024]{1,0:T(8,128)}), f32[1536,1024]{1,0:T(8,128)}) %reduce-scatter.17.cloned.1.call-update) | async-done | bytes 6291472 | tf_op jit(solution)/shard_map/reduce_scatter | solution.py:108
  977.5 79.8 %all-gather.10.cloned.1.call-done = bf16[3072,1024]{1,0:T(8,128)(2,1)} async-done(((bf16[1536,1024]{1,0:T(8,128)(2,1)}), bf16[3072,1024]{1,0:T(8,128)(2,1)}) %all-gather.10.cloned.1.call-update) | async-done | bytes 6291472 | tf_op jit(solution)/shard_map/all_gather | solution.py:115
  1067.3 72.6 %all-gather.12.cloned.1.call-done = bf16[3072,1024]{1,0:T(8,128)(2,1)} async-done(((bf16[1536,1024]{1,0:T(8,128)(2,1)}), bf16[3072,1024]{1,0:T(8,128)(2,1)}) %all-gather.12.cloned.1.call-update) | async-done | bytes 6291472 | tf_op jit(solution)/shard_map/all_gather | solution.py:116
  1150.5 85.4 %reduce-scatter.25.cloned.1.call-done = bf16[768,768]{1,0:T(8,128)(2,1)} async-done(((bf16[3072,768]{1,0:T(8,128)(2,1)}), bf16[768,768]{1,0:T(8,128)(2,1)}) %reduce-scatter.25.cloned.1.call-update) | async-done | bytes 1179664 | tf_op jit(solution)/shard_map/reduce_scatter | solution.py:91
  1251.1 26.9 %collective-permute-done.9 = bf16[768,768]{1,0:T(8,128)(2,1)S(1)} collective-permute-done((bf16[768,768]{1,0:T(8,128)(2,1)S(1)}, bf16[768,768]{1,0:T(8,128)(2,1)S(1)}, u32[]{:S(2)}, u32[]{:S(2)}) %collective-permute-start.9) | collective-permute-done | bytes 1179680 | tf_op jit(solution)/shard_map/ppermute | solution.py:20
  1302.6 23.6 %collective-permute-done.11 = bf16[768,768]{1,0:T(8,128)(2,1)S(1)} collective-permute-done((bf16[768,768]{1,0:T(8,128)(2,1)S(1)}, bf16[768,768]{1,0:T(8,128)(2,1)S(1)}, u32[]{:S(2)}, u32[]{:S(2)}) %collective-permute-start.11) | collective-permute-done | bytes 1179680 | tf_op jit(solution)/shard_map/ppermute | solution.py:20
  1333.1 32.9 %reduce-scatter.27.cloned.1.call-done = bf16[1536,384]{1,0:T(8,128)(2,1)} async-done(((bf16[3072,384]{1,0:T(8,128)(2,1)}), bf16[1536,384]{1,0:T(8,128)(2,1)}) %reduce-scatter.27.cloned.1.call-update) | async-done | bytes 1179664 | tf_op jit(solution)/shard_map/reduce_scatter | solution.py:101
  1368.3 203.4 %while.32 = (s32[]{:T(128)}, f32[1536,6,64]{0,2,1:T(8,128)}, f32[1536,6,64]{0,2,1:T(8,128)}, f32[6,1536]{1,0:T(8,128)S(1)}, bf16[3,512,6,64]{1,3,2,0:T(8,128)(2,...) while((s32[]{:T(128)}, f32[1536,6,64]{0,2,1:T(8,128)}, ...), condition=%wide.region_33.34_spmd.clone, body=%wide.region_29.33_spmd.clone.sunk | while | flops 3093238784 | bytes 276796800 | solution.py:252
  1625.5 46.6 %all-gather.14.cloned.1.call-done = bf16[3072,1152]{0,1:T(8,128)(2,1)} async-done(((bf16[1536,1152]{0,1:T(8,128)(2,1)}), bf16[3072,1152]{0,1:T(8,128)(2,1)}) %all-gather.14.cloned.1.call-update) | async-done | bytes 7077904 | tf_op jit(solution)/shard_map/all_gather | solution.py:115
  1735.8 81.0 %all-reduce.8.cloned.1.call-done = (bf16[768,1152]{1,0:T(8,128)(2,1)}, bf16[384,768]{1,0:T(8,128)(2,1)}, bf16[768,1024]{1,0:T(8,128)(2,1)}, bf16[768,1024]{1,0:T(8,128)(2,1)}, bf16[1024,768]{1,0:T(8,128)(2,1)}) async-done(((bf16[768,1152]{1,0:T(8,128)(2,1)}, bf16[384,768]{1,0:T(8,128)(2,1)}, bf16[768,1024]{1,0:T(8,128)(2,1)}, bf16[768,1024]{1,0:T(8,128)(2,1)}, bf16[1024,768]{1,0:T(8,128)(2,1)}), ...) | async-done | bytes 7077904 | tf_op jit(solution)/shard_map/psum | solution.py:284
  1829.0 75.5 %reduce-scatter.29.cloned.1.call-done = bf16[768,768]{1,0:T(8,128)(2,1)} async-done(((bf16[3072,768]{1,0:T(8,128)(2,1)}), bf16[768,768]{1,0:T(8,128)(2,1)}) %reduce-scatter.29.cloned.1.call-update) | async-done | bytes 1179664 | tf_op jit(solution)/shard_map/reduce_scatter | solution.py:91
  1906.9 36.5 %all-reduce.3 = (f32[768]{0:T(1024)}, f32[768]{0:T(1024)}) all-reduce(f32[768]{0:T(1024)S(1)} %get-tuple-element.219, f32[768]{0:T(1024)S(1)} %copy-done.45), channel_id=1, replica_groups=mesh['dp'=4,'row'=2,'col'=4] {'dp','col'}, use_global_device_ids=true, to_apply=%region_46.47 | all-reduce | flops 1536 | bytes 12288 | tf_op jit(solution)/shard_map/psum | solution.py:282
  1948.2 46.4 %reduce-scatter.21.cloned.1.call-done = bf16[768,768]{1,0:T(8,128)(2,1)} async-done(((bf16[3072,768]{1,0:T(8,128)(2,1)}), bf16[768,768]{1,0:T(8,128)(2,1)}) %reduce-scatter.21.cloned.1.call-update) | async-done | bytes 1179664 | tf_op jit(solution)/shard_map/reduce_scatter | solution.py:91
  (406 shorter events, 679.0 us)
Async XLA Ops:
  7.2 110.9 %reduce-scatter.13.cloned.1.call-start = ((), (), s32[]{:S(2)}) async-start(), calls=%async_computation.11 | async-start | bytes 147456 | tf_op jit(solution)/shard_map/reduce_scatter | solution.py:109
  21.4 53.3 %collective-permute-start.1 = (bf16[768,768]{1,0:T(8,128)(2,1)}, bf16[768,768]{1,0:T(8,128)(2,1)}, u32[]{:S(2)}, u32[]{:S(2)}) collective-permute-start(bf16[768,768]{1,0:T(8,128)(2,1)} %get-tuple-element.286), channel_id=1, source_target_pairs={{0,3},{1,0},{2,1},{3,2},{4,7},{5,4},{6,5},{7,6},{8,11},{9,8},{10,9... | collective-permute-start | bytes 3538952 | tf_op jit(solution)/shard_map/ppermute | solution.py:23
  50.6 48.6 %collective-permute-start.2 = (bf16[768,768]{1,0:T(8,128)(2,1)S(1)}, bf16[768,768]{1,0:T(8,128)(2,1)}, u32[]{:S(2)}, u32[]{:S(2)}) collective-permute-start(bf16[768,768]{1,0:T(8,128)(2,1)S(1)} %collective-permute-done), channel_id=1, source_target_pairs={{0,1},{1,2},{2,3},{3,0},{4,5},{5,6},{6,7},{7,4},{8,9},{9,10},{10,1... | collective-permute-start | bytes 3538952 | tf_op jit(solution)/shard_map/ppermute | solution.py:20
  105.9 173.3 %reduce-scatter.11.cloned.1.call-start = ((), (), s32[]{:S(2)}) async-start(), calls=%async_computation.10 | async-start | bytes 21233664 | tf_op jit(solution)/shard_map/reduce_scatter | solution.py:108
  117.1 294.1 %all-gather.6.cloned.1.call-start = ((), (), s32[]{:S(2)}) async-start(), calls=%async_computation.12 | async-start | bytes 3538944 | tf_op jit(solution)/shard_map/all_gather | solution.py:97
  374.9 206.3 %reduce-scatter.15.cloned.1.call-start = ((), (), s32[]{:S(2)}) async-start(), calls=%async_computation.13 | async-start | bytes 5898240 | tf_op jit(solution)/shard_map/reduce_scatter | solution.py:91
  417.6 269.9 %reduce-scatter.23.cloned.1.call-start = ((), (), s32[]{:S(2)}) async-start(), calls=%async_computation.18 | async-start | bytes 9437184 | tf_op jit(solution)/shard_map/reduce_scatter | solution.py:101
  418.8 52.5 %collective-permute-start.6 = (bf16[768,768]{1,0:T(8,128)(2,1)S(1)}, bf16[768,768]{1,0:T(8,128)(2,1)S(1)}, u32[]{:S(2)}, u32[]{:S(2)}) collective-permute-start(bf16[768,768]{1,0:T(8,128)(2,1)S(1)} %copy-done.11), channel_id=1, source_target_pairs={{0,1},{1,2},{2,3},{3,0},{4,5},{5,6},{6,7},{7,4},{8,9},{9,10},{10,1... | collective-permute-start | bytes 3538952 | tf_op jit(solution)/shard_map/ppermute | solution.py:20
  420.3 107.2 %collective-permute-start.7 = (bf16[768,768]{1,0:T(8,128)(2,1)S(1)}, bf16[768,768]{1,0:T(8,128)(2,1)S(1)}, u32[]{:S(2)}, u32[]{:S(2)}) collective-permute-start(bf16[768,768]{1,0:T(8,128)(2,1)S(1)} %copy-done.11), channel_id=1, source_target_pairs={{0,3},{1,0},{2,1},{3,2},{4,7},{5,4},{6,5},{7,6},{8,11},{9,8},{10,9... | collective-permute-start | bytes 3538952 | tf_op jit(solution)/shard_map/ppermute | solution.py:23
  471.4 100.1 %collective-permute-start.8 = (bf16[768,768]{1,0:T(8,128)(2,1)S(1)}, bf16[768,768]{1,0:T(8,128)(2,1)S(1)}, u32[]{:S(2)}, u32[]{:S(2)}) collective-permute-start(bf16[768,768]{1,0:T(8,128)(2,1)S(1)} %collective-permute-done.6), channel_id=1, source_target_pairs={{0,1},{1,2},{2,3},{3,0},{4,5},{5,6},{6,7},{7,4},{8,9},{9,10},{10,1... | collective-permute-start | bytes 3538952 | tf_op jit(solution)/shard_map/ppermute | solution.py:20
  581.1 238.8 %reduce-scatter.19.cloned.1.call-start = ((), (), s32[]{:S(2)}) async-start(), calls=%async_computation.15 | async-start | bytes 18874368 | tf_op jit(solution)/shard_map/reduce_scatter | solution.py:109
  591.5 53.6 %collective-permute-start.4 = (bf16[768,768]{1,0:T(8,128)(2,1)S(1)}, bf16[768,768]{1,0:T(8,128)(2,1)S(1)}, u32[]{:S(2)}, u32[]{:S(2)}) collective-permute-start(bf16[768,768]{1,0:T(8,128)(2,1)S(1)} %get-tuple-element.284), channel_id=1, source_target_pairs={{0,3},{1,0},{2,1},{3,2},{4,7},{5,4},{6,5},{7,6},{8,11},{9,8},{10,9... | collective-permute-start | bytes 3538952 | tf_op jit(solution)/shard_map/ppermute | solution.py:23
  676.9 289.9 %reduce-scatter.17.cloned.1.call-start = ((), (), s32[]{:S(2)}) async-start(), calls=%async_computation.14 | async-start | bytes 18874368 | tf_op jit(solution)/shard_map/reduce_scatter | solution.py:108
  687.4 369.9 %all-gather.10.cloned.1.call-start = ((), (), s32[]{:S(2)}) async-start(), calls=%async_computation.19 | async-start | bytes 9437184 | tf_op jit(solution)/shard_map/all_gather | solution.py:115
  976.7 163.2 %all-gather.12.cloned.1.call-start = ((), (), s32[]{:S(2)}) async-start(), calls=%async_computation.20 | async-start | bytes 9437184 | tf_op jit(solution)/shard_map/all_gather | solution.py:116
  977.5 258.4 %reduce-scatter.25.cloned.1.call-start = ((), (), s32[]{:S(2)}) async-start(), calls=%async_computation.21 | async-start | bytes 5898240 | tf_op jit(solution)/shard_map/reduce_scatter | solution.py:91
  1150.4 215.5 %reduce-scatter.27.cloned.1.call-start = ((), (), s32[]{:S(2)}) async-start(), calls=%async_computation.22 | async-start | bytes 3538944 | tf_op jit(solution)/shard_map/reduce_scatter | solution.py:101
  1248.7 53.8 %collective-permute-start.10 = (bf16[768,768]{1,0:T(8,128)(2,1)S(1)}, bf16[768,768]{1,0:T(8,128)(2,1)S(1)}, u32[]{:S(2)}, u32[]{:S(2)}) collective-permute-start(bf16[768,768]{1,0:T(8,128)(2,1)S(1)} %get-tuple-element.282), channel_id=1, source_target_pairs={{0,3},{1,0},{2,1},{3,2},{4,7},{5,4},{6,5},{7,6},{8,11},{9,8},{10,9... | collective-permute-start | bytes 3538952 | tf_op jit(solution)/shard_map/ppermute | solution.py:23
  1278.0 48.3 %collective-permute-start.11 = (bf16[768,768]{1,0:T(8,128)(2,1)S(1)}, bf16[768,768]{1,0:T(8,128)(2,1)S(1)}, u32[]{:S(2)}, u32[]{:S(2)}) collective-permute-start(bf16[768,768]{1,0:T(8,128)(2,1)S(1)} %collective-permute-done.9), channel_id=1, source_target_pairs={{0,1},{1,2},{2,3},{3,0},{4,5},{5,6},{6,7},{7,4},{8,9},{9,10},{10,1... | collective-permute-start | bytes 3538952 | tf_op jit(solution)/shard_map/ppermute | solution.py:20
  1332.4 269.9 %all-gather.8.cloned.1.call-start = ((), (), s32[]{:S(2)}) async-start(), calls=%async_computation.16 | async-start | bytes 9437184 | tf_op jit(solution)/shard_map/all_gather | solution.py:97
  1333.0 339.1 %all-gather.14.cloned.1.call-start = ((), (), s32[]{:S(2)}) async-start(), calls=%async_computation.23 | async-start | bytes 10616832 | tf_op jit(solution)/shard_map/all_gather | solution.py:115
  1582.4 234.5 %all-reduce.8.cloned.1.call-start = ((), (), s32[]{:S(2)}) async-start(), calls=%async_computation.25 | async-start | bytes 14155776 | tf_op jit(solution)/shard_map/psum | solution.py:284
  1683.3 221.2 %reduce-scatter.29.cloned.1.call-start = ((), (), s32[]{:S(2)}) async-start(), calls=%async_computation.24 | async-start | bytes 5898240 | tf_op jit(solution)/shard_map/reduce_scatter | solution.py:91
  1708.7 286.0 %reduce-scatter.21.cloned.1.call-start = ((), (), s32[]{:S(2)}) async-start(), calls=%async_computation.17 | async-start | bytes 5898240 | tf_op jit(solution)/shard_map/reduce_scatter | solution.py:91
  (70 other events, 3371.6 us)
Sparse Core Ops, SparseCore 0:
  106.0 9.3 reduce-scatter.12
  117.7 161.4 reduce-scatter.10
  375.0 36.0 all-gather.5
  417.7 157.8 reduce-scatter.14
  581.2 76.4 reduce-scatter.22
  677.0 142.8 reduce-scatter.18
  822.3 144.4 reduce-scatter.16
  976.8 80.3 all-gather.9
  1059.5 80.3 all-gather.11
  1150.5 85.2 reduce-scatter.24
  1332.5 33.3 reduce-scatter.26
  1367.9 80.3 all-gather.7
  1582.5 89.5 all-gather.13
  1683.5 133.3 all-reduce.7
  1819.0 85.4 reduce-scatter.28
  1906.6 87.9 reduce-scatter.20
